TPU v7x, 32 devices: a whole 2x2x4 slice. The times are simulated.
32 devices in a mesh: prow: 8 (over y, x, core), pcol: 4 (over z).
Axes of the slice: x: 2, y: 2, z: 4, core: 2. Of those that a mesh axis runs over, the one named last changes fastest.
Arguments:
- panel: float32 [16, 1024, 128], P('pcol', 'prow'), may hold values from -8 to 192, as said below
- strip: float32 [16, 1024, 2, 512], P(None, 'prow', None, 'pcol'), may hold values from -6 to 6
- factor: float32 [16, 1024, 2, 512], P(None, 'prow', None, 'pcol'), may hold values from -0.125 to 0.125
- inv_diag: float32 [8, 128, 128], replicated, may hold values from -0.24 to 1.4, as said below
- rhs: float32 [16, 1024, 256], P(None, 'prow'), may hold values from -6 to 6
Outputs:
- panel_factor: float32 [16, 1024, 128], P('pcol', 'prow')
- new_strip: float32 [16, 1024, 2, 512], P(None, 'prow', None, 'pcol')
- forward: float32 [16, 1024, 256], P(None, 'prow')
Inputs may be any that keep to these rules, and one draw needn't show every extreme that they name: Row tile 8 of the panel, read as in the first step, is symmetric positive definite. `inv_diag`: every block is lower triangular with a positive diagonal.
All inputs are finite; a program needn't handle non-finite values.
Results may differ from a plain program's by a relative error of at most 0.00018.
Values sent between devices are 32-bit elements; how exact they have to be, the bound alone decides.
A program may use at most 64 MiB of HBM per device.

v0:
```python
import jax
import jax.numpy as jnp
from jax import lax
from jax.sharding import PartitionSpec as P

KF = 2
CTD = 2


def from_root(block, axis, owner):
    block = jnp.where(lax.axis_index(axis) == owner, block, jnp.zeros_like(block))
    return lax.psum(block, axis)


def per_device(panel, strip, factor, inv_diag, rhs):
    highest = lax.Precision.HIGHEST
    grid_rows = lax.axis_size("prow")
    grid_cols = lax.axis_size("pcol")
    row_place = lax.axis_index("prow")
    col_place = lax.axis_index("pcol")
    own_tiles = panel.shape[0]
    tile_size = panel.shape[1]
    tile_rows = strip.shape[0]
    rhs_count = rhs.shape[2]
    sweep_tiles = KF * grid_cols
    strip_tiles = CTD * grid_cols
    diag_row = sweep_tiles // grid_rows
    root_index = sweep_tiles % grid_rows * grid_cols + diag_row // own_tiles
    diag_block = from_root(panel[diag_row % own_tiles], ("prow", "pcol"), root_index)
    diag_factor = jnp.linalg.cholesky(diag_block)
    inverse = jax.scipy.linalg.solve_triangular(
        diag_factor, jnp.eye(tile_size, dtype=jnp.float32), lower=True
    )
    scaled = jnp.einsum("atb,cb->atc", panel, inverse, precision=highest)
    local_tile = (col_place * own_tiles + jnp.arange(own_tiles)) * grid_rows + row_place
    panel_factor = jnp.where((local_tile > sweep_tiles)[:, None, None], scaled, 0.0)
    panel_factor = jnp.where(
        (local_tile == sweep_tiles)[:, None, None], diag_factor[None], panel_factor
    )
    row_factor = lax.all_gather(panel_factor, "pcol", axis=0, tiled=True)
    row_tile = jnp.arange(tile_rows) * grid_rows + row_place
    below_part = jnp.where((row_tile > sweep_tiles)[:, None, None], row_factor, 0.0)
    wanted = sweep_tiles + 1 + jnp.arange(CTD) * grid_cols + col_place
    slot_count = -(-strip_tiles // grid_rows)
    first_slot = (sweep_tiles + grid_rows - row_place) // grid_rows
    outgoing = lax.dynamic_slice_in_dim(below_part, first_slot, slot_count, 0)
    pooled = lax.all_gather(outgoing, "prow", axis=0, tiled=True)
    owner_row = wanted % grid_rows
    slot_place = (
        owner_row * slot_count
        + wanted // grid_rows
        - (sweep_tiles + grid_rows - owner_row) // grid_rows
    )
    column = pooled[slot_place]
    new_strip = strip - jnp.einsum("itb,scb->itsc", below_part, column, precision=highest)
    start_solved = jnp.zeros((sweep_tiles, tile_size, rhs_count), jnp.float32)
    reduce_row = lambda pending: lax.psum(pending, "pcol")
    spread_row = lambda solution, root_row: from_root(solution, "prow", root_row)

    def advance(sweep_step, carried):
        partial_rows, solved, pending = carried
        tile_here = sweep_step // grid_rows
        pending = lax.dynamic_index_in_dim(partial_rows, tile_here, 0, keepdims=False)
        summed = reduce_row(pending)
        residue = lax.dynamic_index_in_dim(rhs, tile_here, 0, keepdims=False) - summed
        diag_inverse = lax.dynamic_index_in_dim(inv_diag, sweep_step, 0, keepdims=False)
        solution = jnp.dot(diag_inverse, residue, precision=highest)
        solution = spread_row(solution, sweep_step % grid_rows)
        solved = lax.dynamic_update_index_in_dim(solved, solution, sweep_step, 0)
        columns = lax.dynamic_index_in_dim(factor, sweep_step // grid_cols, 2, keepdims=False)
        holds_column = col_place == sweep_step % grid_cols
        update = jnp.einsum("itc,cr->itr", columns, solution, precision=highest)
        partial_rows = partial_rows + jnp.where(holds_column, update, 0.0)
        return (partial_rows, solved, pending)

    start_rows = jnp.zeros(rhs.shape, jnp.float32)
    start_pending = jnp.zeros((tile_size, rhs_count), jnp.float32)
    partial_rows, solved, unused_pending = lax.fori_loop(
        0, sweep_tiles, advance, (start_rows, start_solved, start_pending)
    )
    partial_rows, solved = (partial_rows, solved)
    totals = lax.psum(partial_rows, "pcol")
    remains = rhs - totals
    panel_solution = jnp.dot(inverse, remains[sweep_tiles // grid_rows], precision=highest)
    panel_solution = from_root(panel_solution, "prow", sweep_tiles % grid_rows)
    remains = remains - jnp.einsum("itb,br->itr", below_part, panel_solution, precision=highest)
    earlier = solved[jnp.minimum(row_tile, sweep_tiles - 1)]
    forward = jnp.where((row_tile == sweep_tiles)[:, None, None], panel_solution[None], remains)
    forward = jnp.where((row_tile < sweep_tiles)[:, None, None], earlier, forward)
    return (panel_factor, new_strip, forward)


def solution(mesh):
    in_specs = (
        P("pcol", "prow", None),
        P(None, "prow", None, "pcol"),
        P(None, "prow", None, "pcol"),
        P(),
        P(None, "prow", None),
    )
    out_specs = (P("pcol", "prow", None), P(None, "prow", None, "pcol"), P(None, "prow", None))
    return jax.shard_map(
        per_device, mesh=mesh, in_specs=in_specs, out_specs=out_specs, check_vma=False
    )
```

profile of v0, /device:TPU:0, one launch (start us, length us, event | category | flops | bytes accessed | tf_op | source)
XLA Modules:
  0.0 1144.2 jit_solution(4040450262911026411)
XLA Ops:
  8.9 125.6 %all-reduce.6.cloned.1.call-done = f32[128,128]{0,1:T(8,128)} async-done(((f32[128,128]{0,1:T(8,128)}), f32[128,128]{0,1:T(8,128)}) %all-reduce.6.cloned.1.call-update) | async-done | bytes 65552 | tf_op jit(solution)/shard_map/psum | solution.py:12
  136.2 11.7 %cholesky.19 = f32[128,128]{1,0:T(8,128)S(1)} custom-call(f32[128,128]{1,0:T(8,128)S(1)} %fusion.13), custom_call_target="Cholesky" | custom-call | tf_op jit(solution)/shard_map/jit(cholesky)/cholesky | solution.py:30
  149.3 9.8 custom-call.7
  161.6 796.4 %while.19 = (s32[]{:T(128)}, f32[16,128,256]{2,1,0:T(8,128)}, f32[8,128,256]{2,1,0:T(8,128)}, s32[]{:T(128)}, f32[16,128,2,128]{3,2,1,0:T(2,128)}, /*index=5*/f3...) while((s32[]{:T(128)}, f32[16,128,256]{2,1,0:T(8,128)}, ...), condition=%wide.region_6.7_spmd.clone, body=%wide.region_3.6_spmd.clone.sunk | while | flops 857342016 | bytes 14221928 | solution.py:78
  162.6 38.0 %all-reduce.12.cloned.1.call-done = f32[128,256]{1,0:T(8,128)} async-done(((f32[128,256]{1,0:T(8,128)}), f32[128,256]{1,0:T(8,128)}) %all-reduce.12.cloned.1.call-update) | async-done | bytes 131088 | tf_op jit(solution)/shard_map/while/body/eval_jaxpr/psum | solution.py:57
  205.3 51.9 %all-reduce.14.cloned.1.call-done = f32[128,256]{1,0:T(8,128)} async-done(((f32[128,256]{1,0:T(8,128)}), f32[128,256]{1,0:T(8,128)}) %all-reduce.14.cloned.1.call-update) | async-done | bytes 131088 | tf_op jit(solution)/shard_map/while/body/eval_jaxpr/psum | solution.py:12
  265.3 34.7 %all-reduce.12.cloned.1.call-done = f32[128,256]{1,0:T(8,128)} async-done(((f32[128,256]{1,0:T(8,128)}), f32[128,256]{1,0:T(8,128)}) %all-reduce.12.cloned.1.call-update) | async-done | bytes 131088 | tf_op jit(solution)/shard_map/while/body/eval_jaxpr/psum | solution.py:57
  304.7 51.7 %all-reduce.14.cloned.1.call-done = f32[128,256]{1,0:T(8,128)} async-done(((f32[128,256]{1,0:T(8,128)}), f32[128,256]{1,0:T(8,128)}) %all-reduce.14.cloned.1.call-update) | async-done | bytes 131088 | tf_op jit(solution)/shard_map/while/body/eval_jaxpr/psum | solution.py:12
  364.5 34.7 %all-reduce.12.cloned.1.call-done = f32[128,256]{1,0:T(8,128)} async-done(((f32[128,256]{1,0:T(8,128)}), f32[128,256]{1,0:T(8,128)}) %all-reduce.12.cloned.1.call-update) | async-done | bytes 131088 | tf_op jit(solution)/shard_map/while/body/eval_jaxpr/psum | solution.py:57
  403.9 51.9 %all-reduce.14.cloned.1.call-done = f32[128,256]{1,0:T(8,128)} async-done(((f32[128,256]{1,0:T(8,128)}), f32[128,256]{1,0:T(8,128)}) %all-reduce.14.cloned.1.call-update) | async-done | bytes 131088 | tf_op jit(solution)/shard_map/while/body/eval_jaxpr/psum | solution.py:12
  463.9 35.0 %all-reduce.12.cloned.1.call-done = f32[128,256]{1,0:T(8,128)} async-done(((f32[128,256]{1,0:T(8,128)}), f32[128,256]{1,0:T(8,128)}) %all-reduce.12.cloned.1.call-update) | async-done | bytes 131088 | tf_op jit(solution)/shard_map/while/body/eval_jaxpr/psum | solution.py:57
  503.5 51.9 %all-reduce.14.cloned.1.call-done = f32[128,256]{1,0:T(8,128)} async-done(((f32[128,256]{1,0:T(8,128)}), f32[128,256]{1,0:T(8,128)}) %all-reduce.14.cloned.1.call-update) | async-done | bytes 131088 | tf_op jit(solution)/shard_map/while/body/eval_jaxpr/psum | solution.py:12
  563.6 34.6 %all-reduce.12.cloned.1.call-done = f32[128,256]{1,0:T(8,128)} async-done(((f32[128,256]{1,0:T(8,128)}), f32[128,256]{1,0:T(8,128)}) %all-reduce.12.cloned.1.call-update) | async-done | bytes 131088 | tf_op jit(solution)/shard_map/while/body/eval_jaxpr/psum | solution.py:57
  602.8 51.9 %all-reduce.14.cloned.1.call-done = f32[128,256]{1,0:T(8,128)} async-done(((f32[128,256]{1,0:T(8,128)}), f32[128,256]{1,0:T(8,128)}) %all-reduce.14.cloned.1.call-update) | async-done | bytes 131088 | tf_op jit(solution)/shard_map/while/body/eval_jaxpr/psum | solution.py:12
  662.9 34.7 %all-reduce.12.cloned.1.call-done = f32[128,256]{1,0:T(8,128)} async-done(((f32[128,256]{1,0:T(8,128)}), f32[128,256]{1,0:T(8,128)}) %all-reduce.12.cloned.1.call-update) | async-done | bytes 131088 | tf_op jit(solution)/shard_map/while/body/eval_jaxpr/psum | solution.py:57
  702.2 51.9 %all-reduce.14.cloned.1.call-done = f32[128,256]{1,0:T(8,128)} async-done(((f32[128,256]{1,0:T(8,128)}), f32[128,256]{1,0:T(8,128)}) %all-reduce.14.cloned.1.call-update) | async-done | bytes 131088 | tf_op jit(solution)/shard_map/while/body/eval_jaxpr/psum | solution.py:12
  762.2 34.6 %all-reduce.12.cloned.1.call-done = f32[128,256]{1,0:T(8,128)} async-done(((f32[128,256]{1,0:T(8,128)}), f32[128,256]{1,0:T(8,128)}) %all-reduce.12.cloned.1.call-update) | async-done | bytes 131088 | tf_op jit(solution)/shard_map/while/body/eval_jaxpr/psum | solution.py:57
  801.5 51.7 %all-reduce.14.cloned.1.call-done = f32[128,256]{1,0:T(8,128)} async-done(((f32[128,256]{1,0:T(8,128)}), f32[128,256]{1,0:T(8,128)}) %all-reduce.14.cloned.1.call-update) | async-done | bytes 131088 | tf_op jit(solution)/shard_map/while/body/eval_jaxpr/psum | solution.py:12
  861.4 34.7 %all-reduce.12.cloned.1.call-done = f32[128,256]{1,0:T(8,128)} async-done(((f32[128,256]{1,0:T(8,128)}), f32[128,256]{1,0:T(8,128)}) %all-reduce.12.cloned.1.call-update) | async-done | bytes 131088 | tf_op jit(solution)/shard_map/while/body/eval_jaxpr/psum | solution.py:57
  900.7 51.7 %all-reduce.14.cloned.1.call-done = f32[128,256]{1,0:T(8,128)} async-done(((f32[128,256]{1,0:T(8,128)}), f32[128,256]{1,0:T(8,128)}) %all-reduce.14.cloned.1.call-update) | async-done | bytes 131088 | tf_op jit(solution)/shard_map/while/body/eval_jaxpr/psum | solution.py:12
  961.5 26.5 %all-gather.2.cloned.1.call-done = f32[16,128,128]{2,1,0:T(8,128)} async-done(((f32[4,128,128]{2,1,0:T(8,128)}), f32[16,128,128]{2,1,0:T(8,128)}) %all-gather.2.cloned.1.call-update) | async-done | bytes 1048592 | tf_op jit(solution)/shard_map/all_gather | solution.py:40
  989.4 10.0 all_gather.7
  1000.0 77.0 %all-reduce.8.cloned.1.call-done = f32[16,128,256]{2,1,0:T(8,128)} async-done(((f32[16,128,256]{2,1,0:T(8,128)}), f32[16,128,256]{2,1,0:T(8,128)}) %all-reduce.8.cloned.1.call-update) | async-done | bytes 2097168 | tf_op jit(solution)/shard_map/psum | solution.py:82
  1086.8 45.9 %all-reduce.10.cloned.1.call-done = f32[128,256]{1,0:T(8,128)} async-done(((f32[128,256]{1,0:T(8,128)}), f32[128,256]{1,0:T(8,128)}) %all-reduce.10.cloned.1.call-update) | async-done | bytes 131088 | tf_op jit(solution)/shard_map/psum | solution.py:12
  (120 shorter events, 127.4 us)
Async XLA Ops:
  7.2 127.3 %all-reduce.6.cloned.1.call-start = ((), (), s32[]{:S(2)}) async-start(), calls=%async_computation | async-start | bytes 131072 | tf_op jit(solution)/shard_map/psum | solution.py:12
  161.6 39.0 %all-reduce.12.cloned.1.call-start = ((), (), s32[]{:S(2)}) async-start(), calls=%async_computation.4 | async-start | bytes 262144 | tf_op jit(solution)/shard_map/while/body/eval_jaxpr/psum | solution.py:57
  162.6 94.6 %all-reduce.14.cloned.1.call-start = ((), (), s32[]{:S(2)}) async-start(), calls=%async_computation.5 | async-start | bytes 262144 | tf_op jit(solution)/shard_map/while/body/eval_jaxpr/psum | solution.py:12
  262.7 37.3 %all-reduce.12.cloned.1.call-start = ((), (), s32[]{:S(2)}) async-start(), calls=%async_computation.4 | async-start | bytes 262144 | tf_op jit(solution)/shard_map/while/body/eval_jaxpr/psum | solution.py:57
  265.3 91.1 %all-reduce.14.cloned.1.call-start = ((), (), s32[]{:S(2)}) async-start(), calls=%async_computation.5 | async-start | bytes 262144 | tf_op jit(solution)/shard_map/while/body/eval_jaxpr/psum | solution.py:12
  361.9 37.3 %all-reduce.12.cloned.1.call-start = ((), (), s32[]{:S(2)}) async-start(), calls=%async_computation.4 | async-start | bytes 262144 | tf_op jit(solution)/shard_map/while/body/eval_jaxpr/psum | solution.py:57
  364.5 91.3 %all-reduce.14.cloned.1.call-start = ((), (), s32[]{:S(2)}) async-start(), calls=%async_computation.5 | async-start | bytes 262144 | tf_op jit(solution)/shard_map/while/body/eval_jaxpr/psum | solution.py:12
  461.3 37.5 %all-reduce.12.cloned.1.call-start = ((), (), s32[]{:S(2)}) async-start(), calls=%async_computation.4 | async-start | bytes 262144 | tf_op jit(solution)/shard_map/while/body/eval_jaxpr/psum | solution.py:57
  463.8 91.6 %all-reduce.14.cloned.1.call-start = ((), (), s32[]{:S(2)}) async-start(), calls=%async_computation.5 | async-start | bytes 262144 | tf_op jit(solution)/shard_map/while/body/eval_jaxpr/psum | solution.py:12
  561.0 37.2 %all-reduce.12.cloned.1.call-start = ((), (), s32[]{:S(2)}) async-start(), calls=%async_computation.4 | async-start | bytes 262144 | tf_op jit(solution)/shard_map/while/body/eval_jaxpr/psum | solution.py:57
  563.5 91.2 %all-reduce.14.cloned.1.call-start = ((), (), s32[]{:S(2)}) async-start(), calls=%async_computation.5 | async-start | bytes 262144 | tf_op jit(solution)/shard_map/while/body/eval_jaxpr/psum | solution.py:12
  660.3 37.3 %all-reduce.12.cloned.1.call-start = ((), (), s32[]{:S(2)}) async-start(), calls=%async_computation.4 | async-start | bytes 262144 | tf_op jit(solution)/shard_map/while/body/eval_jaxpr/psum | solution.py:57
  662.8 91.3 %all-reduce.14.cloned.1.call-start = ((), (), s32[]{:S(2)}) async-start(), calls=%async_computation.5 | async-start | bytes 262144 | tf_op jit(solution)/shard_map/while/body/eval_jaxpr/psum | solution.py:12
  759.6 37.2 %all-reduce.12.cloned.1.call-start = ((), (), s32[]{:S(2)}) async-start(), calls=%async_computation.4 | async-start | bytes 262144 | tf_op jit(solution)/shard_map/while/body/eval_jaxpr/psum | solution.py:57
  762.2 91.1 %all-reduce.14.cloned.1.call-start = ((), (), s32[]{:S(2)}) async-start(), calls=%async_computation.5 | async-start | bytes 262144 | tf_op jit(solution)/shard_map/while/body/eval_jaxpr/psum | solution.py:12
  858.8 37.3 %all-reduce.12.cloned.1.call-start = ((), (), s32[]{:S(2)}) async-start(), calls=%async_computation.4 | async-start | bytes 262144 | tf_op jit(solution)/shard_map/while/body/eval_jaxpr/psum | solution.py:57
  861.3 91.1 %all-reduce.14.cloned.1.call-start = ((), (), s32[]{:S(2)}) async-start(), calls=%async_computation.5 | async-start | bytes 262144 | tf_op jit(solution)/shard_map/while/body/eval_jaxpr/psum | solution.py:12
  958.0 1.4 copy-start
  958.0 30.0 %all-gather.2.cloned.1.call-start = ((), (), s32[]{:S(2)}) async-start(), calls=%async_computation.1 | async-start | bytes 1310720 | tf_op jit(solution)/shard_map/all_gather | solution.py:40
  958.6 118.4 %all-reduce.8.cloned.1.call-start = ((), (), s32[]{:S(2)}) async-start(), calls=%async_computation.2 | async-start | bytes 4194304 | tf_op jit(solution)/shard_map/psum | solution.py:82
  959.3 173.4 %all-reduce.10.cloned.1.call-start = ((), (), s32[]{:S(2)}) async-start(), calls=%async_computation.3 | async-start | bytes 262144 | tf_op jit(solution)/shard_map/psum | solution.py:12
Sparse Core Ops, SparseCore 0:
  14.2 120.2 all-reduce.5
  165.4 35.2 all-reduce.11
  204.6 52.5 all-reduce.13
  266.1 33.8 all-reduce.11
  303.8 52.5 all-reduce.13
  365.3 33.8 all-reduce.11
  403.1 52.5 all-reduce.13
  465.0 33.7 all-reduce.11
  502.8 52.5 all-reduce.13
  564.4 33.7 all-reduce.11
  602.1 52.5 all-reduce.13
  663.7 33.8 all-reduce.11
  701.5 52.5 all-reduce.13
  763.0 33.7 all-reduce.11
  800.6 52.5 all-reduce.13
  862.2 33.8 all-reduce.11
  899.8 52.5 all-reduce.13
  960.7 27.2 all-gather.1
  990.9 86.0 all-reduce.7
  1080.7 51.9 all-reduce.9
where the time goes:
time: 1150 us; the launch traced here: 1140 us
  waiting for transfers between devices  972 us (85%)
  matrix products  58 us (5%)
  local copies, waits for them, and re-layouts  47.7 us (4%)
  other arithmetic  41.2 us (4%)
  between operations  14.2 us (1%)
    psum x10, waiting for transfers between devices, from_root(): return lax.psum(block, axis)  586 us
    psum x8, waiting for transfers between devices, per_device(): reduce_row = lambda pending: lax.psum(pending, 'pcol')  281 us
    psum x1, waiting for transfers between devices, per_device(): totals = lax.psum(partial_rows, 'pcol')  77 us
    dot_general x8, matrix products, advance(): update = jnp.einsum('itc,cr->itr', columns, solution, precision=highest)  32.1 us
    all_gather x1, waiting for transfers between devices, per_device(): row_factor = lax.all_gather(panel_factor, 'pcol', axis=0, tiled=True)  26.5 us
  transfers between devices with their start and end apart: 20, of which 20 were waited for; matrix products, arithmetic and copies ran while one was open for 3% of the time, Pallas kernels for 0%

commit v1 on v0

v1 whole, which is shorter than its diff:
```python
import functools

import jax
import jax.numpy as jnp
from jax import lax
from jax.experimental import pallas as pl
from jax.experimental.pallas import tpu as pltpu
from jax.sharding import PartitionSpec as P

HIGHEST = lax.Precision.HIGHEST
MESH = pl.DeviceIdType.MESH


def dot(a, b):
    return jnp.dot(a, b, precision=HIGHEST, preferred_element_type=jnp.float32)


def when(cond, body):
    if cond is True:
        body()
    else:
        pl.when(cond)(body)


def kernel(
    R, C,
    panel, strip, factor, inv_diag, rhs,
    panel_out, strip_out, forward,
    pan_all, diag, col, ftri, brow, y, frow, tri, inv, inv_t,
    z_send, z_recv, p_send, p_recv, a_send, a_recv, local_sem,
):
    r = lax.axis_index("prow")
    c = lax.axis_index("pcol")
    A, TILE, _ = panel.shape
    KF = factor.shape[0]
    CTD = strip.shape[0]
    I = factor.shape[1]
    KS = KF * C
    NR = rhs.shape[2]
    full = KS == R

    def target(row):
        return jnp.where(row == 0, KS, row) if full else row

    def has_row(row):
        return True if full else jnp.logical_and(row >= 1, row <= KS)

    def slot(row):
        return target(row) if full else jnp.minimum(row, KS)

    first = jnp.where(r == 0, KS // R, 0) if full else 0

    barrier = pltpu.get_barrier_semaphore()

    @pl.loop(1, C)
    def _(d):
        pl.semaphore_signal(barrier, inc=1, device_id={"pcol": lax.rem(c + d, C)}, device_id_type=MESH)

    @pl.loop(1, R)
    def _(d):
        pl.semaphore_signal(barrier, inc=1, device_id={"prow": lax.rem(r + d, R)}, device_id_type=MESH)

    pl.semaphore_wait(barrier, C - 1 + R - 1)

    def z_copy(kind, d, source, place):
        if kind == 0:
            src, dst = factor.at[:, first], ftri.at[slot(r), :, source]
        elif kind == 1:
            src, dst = panel, pan_all.at[pl.ds(source * A, A)]
        else:
            src, dst = factor.at[:, pl.ds(place * A, A)], frow.at[:, source]
        return pltpu.make_async_remote_copy(
            src_ref=src, dst_ref=dst, send_sem=z_send.at[kind, d - 1], recv_sem=z_recv.at[kind, d - 1],
            device_id={"pcol": place}, device_id_type=MESH,
        )

    def z_cond(kind):
        return has_row(r) if kind == 0 else True

    def z_each(kind, act):
        for d in range(1, C):
            when(z_cond(kind), lambda d=d: act(d))

    def z_start(kind):
        z_each(kind, lambda d: z_copy(kind, d, c, lax.rem(c + d, C)).start())

    def z_wait_send(kind):
        z_each(kind, lambda d: z_copy(kind, d, c, lax.rem(c + d, C)).wait_send())

    def z_wait_recv(kind):
        z_each(kind, lambda d: z_copy(kind, d, lax.rem(c + C - d, C), c).wait_recv())

    def wanted(s):
        return KS + 1 + s * C + c

    def p_copy(kind, d, row):
        if kind == 0:
            src, dst = rhs.at[0], brow.at[jnp.minimum(row, KS - 1)]
        elif kind == 1:
            src, dst = rhs.at[KS // R], brow.at[KS]
        elif kind == 2:
            src, dst = pan_all.at[KS // R], diag
        elif kind < 3 + CTD:
            s = kind - 3
            src, dst = pan_all.at[wanted(s) // R], col.at[s]
        else:
            s = kind - 3 - CTD
            src, dst = ftri.at[slot(row), s], ftri.at[slot(row), s]
        return pltpu.make_async_remote_copy(
            src_ref=src, dst_ref=dst, send_sem=p_send.at[kind, d - 1], recv_sem=p_recv.at[kind, d - 1],
            device_id={"prow": lax.rem(r + d, R)}, device_id_type=MESH,
        )

    def p_cond(kind, row):
        if kind == 0:
            return True if full else row < KS
        if kind <= 2:
            return row == KS % R
        if kind < 3 + CTD:
            return row == lax.rem(wanted(kind - 3), R)
        s = kind - 3 - CTD
        if full and s == 0:
            return True
        deep = target(row) > s * C
        return deep if full else jnp.logical_and(deep, row <= KS)

    def p_start(kinds):
        @pl.loop(1, R)
        def _(d):
            for kind in kinds:
                when(p_cond(kind, r), lambda kind=kind: p_copy(kind, d, r).start())

    def p_wait_send(kinds):
        @pl.loop(1, R)
        def _(d):
            for kind in kinds:
                when(p_cond(kind, r), lambda kind=kind: p_copy(kind, d, r).wait_send())

    def p_wait_recv(kinds):
        @pl.loop(1, R)
        def _(d):
            row = lax.rem(r + R - d, R)
            for kind in kinds:
                when(p_cond(kind, row), lambda kind=kind: p_copy(kind, d, row).wait_recv())

    row_kinds = tuple(range(3 + CTD, 3 + CTD + KF))

    z_start(0)
    p_start((0, 1))
    z_start(1)
    z_start(2)

    own = pltpu.make_async_copy(factor.at[:, pl.ds(c * A, A)], frow.at[:, c], local_sem)
    own.start()

    def keep_row():
        ftri[slot(r), :, c] = factor[:, first]

    when(has_row(r), keep_row)
    pan_all[pl.ds(c * A, A)] = panel[...]

    def keep_rhs():
        brow[jnp.minimum(r, KS - 1)] = rhs[0]

    when(p_cond(0, r), keep_rhs)

    @pl.when(p_cond(1, r))
    def _():
        brow[KS] = rhs[KS // R]

    z_wait_recv(0)
    p_start(row_kinds)
    z_wait_recv(1)
    p_start(tuple(range(2, 3 + CTD)))

    @pl.when(p_cond(2, r))
    def _():
        diag[...] = pan_all[KS // R]

    for s in range(CTD):
        @pl.when(p_cond(3 + s, r))
        def _(s=s):
            col[s] = pan_all[wanted(s) // R]

    p_wait_recv((2,))
    lanes = lax.broadcasted_iota(jnp.int32, (TILE, TILE), 1)
    rows = lax.broadcasted_iota(jnp.int32, (TILE, TILE), 0)
    tri[...] = diag[...]
    inv[...] = jnp.where(lanes == rows, 1.0, 0.0)

    def eliminate(k, carry):
        lane = lanes[0:1]
        row = tri[pl.ds(k, 1), :]
        whole = tri[...]
        pivot = jnp.sum(jnp.where(lane == k, row, 0.0), axis=1, keepdims=True)
        scale = 1.0 / jnp.sqrt(pivot)
        lrow = jnp.where(lane >= k, row * scale, 0.0)
        column = jnp.sum(jnp.where(lanes == k, whole, 0.0), axis=1, keepdims=True)
        lcol = jnp.where(rows[:, 0:1] > k, column * scale, 0.0)
        wrow = inv[pl.ds(k, 1), :] * scale
        tri[...] = whole - lcol * lrow
        inv[...] = inv[...] - lcol * wrow
        tri[pl.ds(k, 1), :] = lrow
        inv[pl.ds(k, 1), :] = wrow
        return carry

    lax.fori_loop(0, TILE, eliminate, 0)
    inv_t[...] = inv[...].T

    p_wait_recv((0, 1) + row_kinds)

    def advance(t, carry):
        y[t] = dot(inv_diag[t], brow[t])

        def update(row, carry):
            brow[row] = brow[row] - dot(ftri[row, t // C, lax.rem(t, C)], y[t])
            return carry

        return lax.fori_loop(t + 1, KS + 1, update, carry)

    lax.fori_loop(0, KS, advance, 0)
    panel_solution = dot(inv[...], brow[KS])

    scaled = dot(panel[...].reshape(A * TILE, TILE), inv_t[...])
    for a in range(A):
        tile = (c * A + a) * R + r
        panel_out[a] = jnp.where(tile > KS, scaled[a * TILE:(a + 1) * TILE], 0.0)
    brow[KS] = panel_solution

    z_wait_recv(2)
    own.wait()

    mine = pl.ds(c * A, A)
    below = panel_out[...].reshape(A * TILE, TILE)
    forward[mine] = rhs[mine] - dot(below, brow[KS]).reshape(A, TILE, NR)

    def reach(j, carry):
        part = dot(frow[j // C, lax.rem(j, C)].reshape(A * TILE, TILE), y[j])
        forward[mine] = forward[mine] - part.reshape(A, TILE, NR)
        return carry

    lax.fori_loop(0, KS, reach, 0)

    def settle(a, carry):
        tile = (c * A + a) * R + r

        @pl.when(tile < KS)
        def _():
            forward[c * A + a] = y[jnp.minimum(tile, KS - 1)]

        @pl.when(tile == KS)
        def _():
            forward[c * A + a] = brow[KS]
            panel_out[a] = tri[...].T

        return carry

    lax.fori_loop(0, A, settle, 0)

    def a_copy(d, source, place):
        span = pl.ds(source * A, A)
        return pltpu.make_async_remote_copy(
            src_ref=forward.at[span], dst_ref=forward.at[span],
            send_sem=a_send.at[d - 1], recv_sem=a_recv.at[d - 1],
            device_id={"pcol": place}, device_id_type=MESH,
        )

    for d in range(1, C):
        a_copy(d, c, lax.rem(c + d, C)).start()

    p_wait_recv(tuple(range(3, 3 + CTD)))
    for s in range(CTD):
        col[s] = dot(col[s], inv_t[...]).T

    def strip_row(i, carry):
        tile = i * R + r
        scaled = jnp.where(tile > KS, dot(pan_all[i], inv_t[...]), 0.0)
        for s in range(CTD):
            strip_out[s, i] = strip[s, i] - dot(scaled, col[s])
        return carry

    lax.fori_loop(0, I, strip_row, 0)

    for kind in range(3):
        z_wait_send(kind)
    p_wait_send(tuple(range(3 + CTD + KF)))
    for d in range(1, C):
        a_copy(d, lax.rem(c + C - d, C), c).wait_recv()
    for d in range(1, C):
        a_copy(d, c, lax.rem(c + d, C)).wait_send()


def per_device(panel, strip, factor, inv_diag, rhs):
    R = lax.axis_size("prow")
    C = lax.axis_size("pcol")
    A, TILE, _ = panel.shape
    I, _, CTD, _ = strip.shape
    KF = factor.shape[2]
    NR = rhs.shape[2]
    KS = KF * C
    assert KS <= R
    f32 = jnp.float32
    strip = jnp.transpose(strip, (2, 0, 1, 3))
    factor = jnp.transpose(factor, (2, 0, 1, 3))
    kinds = 3 + CTD + KF
    dma = pltpu.SemaphoreType.DMA
    panel_factor, new_strip, forward = pl.pallas_call(
        functools.partial(kernel, R, C),
        out_shape=(
            jax.ShapeDtypeStruct(panel.shape, f32),
            jax.ShapeDtypeStruct(strip.shape, f32),
            jax.ShapeDtypeStruct(rhs.shape, f32),
        ),
        in_specs=[pl.BlockSpec(memory_space=pltpu.VMEM)] * 5,
        out_specs=[pl.BlockSpec(memory_space=pltpu.VMEM)] * 3,
        scratch_shapes=[
            pltpu.VMEM((I, TILE, TILE), f32),
            pltpu.VMEM((TILE, TILE), f32),
            pltpu.VMEM((CTD, TILE, TILE), f32),
            pltpu.VMEM((KS + 1, KF, C, TILE, TILE), f32),
            pltpu.VMEM((KS + 1, TILE, NR), f32),
            pltpu.VMEM((KS, TILE, NR), f32),
            pltpu.VMEM((KF, C, A, TILE, TILE), f32),
            pltpu.VMEM((TILE, TILE), f32),
            pltpu.VMEM((TILE, TILE), f32),
            pltpu.VMEM((TILE, TILE), f32),
            dma((3, C - 1)),
            dma((3, C - 1)),
            dma((kinds, R - 1)),
            dma((kinds, R - 1)),
            dma((C - 1,)),
            dma((C - 1,)),
            dma,
        ],
        compiler_params=pltpu.CompilerParams(
            collective_id=0, has_side_effects=True, vmem_limit_bytes=56 << 20
        ),
    )(panel, strip, factor, inv_diag, rhs)
    return panel_factor, jnp.transpose(new_strip, (1, 2, 0, 3)), forward


def solution(mesh):
    in_specs = (
        P("pcol", "prow", None),
        P(None, "prow", None, "pcol"),
        P(None, "prow", None, "pcol"),
        P(),
        P(None, "prow", None),
    )
    out_specs = (P("pcol", "prow", None), P(None, "prow", None, "pcol"), P(None, "prow", None))
    return jax.shard_map(
        per_device, mesh=mesh, in_specs=in_specs, out_specs=out_specs, check_vma=False
    )
```

time: 1150 us -> 163 us (0.14)
  the two profiles are of different devices: /device:TPU:0 before, /device:TPU:29 now
where the time goes in v1:
time: 163 us
  Pallas kernels  151 us (93%)
  local copies, waits for them, and re-layouts  11.5 us (7%)
    pallas_call x1, Pallas kernels, per_device(): pl.pallas_call(functools.partial(kernel, R, C), out_shape=(jax.ShapeDtype...  151 us
    unnamed x7, local copies, waits for them, and re-layouts  6.72 us
    transpose x1, local copies, waits for them, and re-layouts, per_device(): factor = jnp.transpose(factor, (2, 0, 1, 3))  4.8 us

profile of v1, /device:TPU:29, one launch (start us, length us, event | category | flops | bytes accessed | tf_op | source)
XLA Modules:
  0.0 163.2 jit_solution(6803337120362906144)
XLA Ops:
  0.6 4.8 %copy_bitcast_fusion = (f32[2,16,128,128]{3,2,1,0:T(8,128)}, f32[2,16,128,128]{3,2,1,0:T(8,128)}) fusion(f32[16,128,2,128]{3,2,1,0:T(2,128)} %param.7, f32[16,128,2,128]{3,2,1,0:T(2,128)} %param.6), kind=kLoop, calls=%fused_computation | loop fusion | bytes 8388608 | tf_op jit(solution)/shard_map/transpose | solution.py:304
  5.4 151.1 %shard_map.76 = (f32[4,128,128]{2,1,0:T(8,128)}, f32[2,16,128,128]{3,2,1,0:T(8,128)}, f32[16,128,256]{2,1,0:T(8,128)}) custom-call(f32[4,128,128]{2,1,0:T(8,128)} %panel.1, f32[2,16,128,128]{3,2,1,0:T(8,128)} %get-tuple-element.13.strip, f32[2,16,128,128]{3,2,1,0:T(8,128)} %get-tuple-element.12.factor, f32[8,128,128]{2,1,0:T(8,128)} %inv_diag.1, ...), custom_call_target="tpu_custom_call" | custom-call | tf_op jit(solution)/shard_map/pallas_call | solution.py:307
  156.5 0.0 copy-start.1
  156.5 0.0 copy-start
  156.5 4.7 %copy.10 = f32[16,128,2,128]{3,2,1,0:T(2,128)} copy(f32[16,128,2,128]{3,1,0,2:T(8,128)} %bitcast.5) | data formatting | bytes 4194304
  161.2 0.0 copy-done.1
  161.2 0.7 copy.15
  161.9 0.0 copy-done
  161.9 1.3 copy.16
Async XLA Ops:
  156.5 4.7 %copy-start.1 = (f32[4,128,128]{2,1,0:T(8,128)S(1)}, f32[4,128,128]{2,1,0:T(8,128)}, u32[]{:S(2)}) copy-start(f32[4,128,128]{2,1,0:T(8,128)} %get-tuple-element.17) | copy-start | bytes 786436
  156.5 5.4 %copy-start = (f32[16,128,256]{2,1,0:T(8,128)S(1)}, f32[16,128,256]{2,1,0:T(8,128)}, u32[]{:S(2)}) copy-start(f32[16,128,256]{2,1,0:T(8,128)} %get-tuple-element.19) | copy-start | bytes 6291460

commit v2 on v1

v2 whole, which is shorter than its diff:
```python
import functools

import jax
import jax.numpy as jnp
from jax import lax
from jax.experimental import pallas as pl
from jax.experimental.pallas import tpu as pltpu
from jax.sharding import PartitionSpec as P

HIGHEST = lax.Precision.HIGHEST
MESH = pl.DeviceIdType.MESH


def dot(a, b):
    return jnp.dot(a, b, precision=HIGHEST, preferred_element_type=jnp.float32)


def when(cond, body):
    if cond is True:
        body()
    else:
        pl.when(cond)(body)


def kernel(
    R, C,
    panel, strip, factor, inv_diag, rhs,
    panel_out, strip_out, forward,
    pan_all, diag, col, ftri, brow, y, frow, tri, inv, inv_t,
    z_send, z_recv, p_send, p_recv, f_send, a_send, a_recv, local_sem,
):
    r = lax.axis_index("prow")
    c = lax.axis_index("pcol")
    A, TILE, _ = panel.shape
    KF = factor.shape[0]
    CTD = strip.shape[0]
    I = factor.shape[1]
    KS = KF * C
    NR = rhs.shape[2]
    full = KS == R

    def target(row):
        return jnp.where(row == 0, KS, row) if full else row

    def has_row(row):
        return True if full else jnp.logical_and(row >= 1, row <= KS)

    def slot(row):
        return target(row) if full else jnp.minimum(row, KS)

    first = jnp.where(r == 0, KS // R, 0) if full else 0

    barrier = pltpu.get_barrier_semaphore()

    @pl.loop(1, C)
    def _(d):
        pl.semaphore_signal(barrier, inc=1, device_id={"pcol": lax.rem(c + d, C)}, device_id_type=MESH)

    @pl.loop(1, R)
    def _(d):
        pl.semaphore_signal(barrier, inc=1, device_id={"prow": lax.rem(r + d, R)}, device_id_type=MESH)

    pl.semaphore_wait(barrier, C - 1 + R - 1)

    def z_copy(kind, d, source, place):
        if kind < KF:
            src, dst = factor.at[kind, first], ftri.at[slot(r), kind * C + source]
        elif kind == KF:
            src, dst = panel, pan_all.at[pl.ds(source * A, A)]
        else:
            src, dst = factor.at[:, pl.ds(place * A, A)], frow.at[:, source]
        return pltpu.make_async_remote_copy(
            src_ref=src, dst_ref=dst, send_sem=z_send.at[kind, d - 1], recv_sem=z_recv.at[kind, d - 1],
            device_id={"pcol": place}, device_id_type=MESH,
        )

    def tiles_of(row):
        return target(row) if full else jnp.where(row <= KS, row, 0)

    def z_cond(kind, source):
        return kind * C + source < tiles_of(r) if kind < KF else True

    def z_start(kind):
        for d in range(1, C):
            when(z_cond(kind, c), lambda d=d: z_copy(kind, d, c, lax.rem(c + d, C)).start())

    def z_wait_send(kind):
        for d in range(1, C):
            when(z_cond(kind, c), lambda d=d: z_copy(kind, d, c, lax.rem(c + d, C)).wait_send())

    def z_wait_recv(kind):
        for d in range(1, C):
            source = lax.rem(c + C - d, C)
            when(z_cond(kind, source), lambda d=d, source=source: z_copy(kind, d, source, c).wait_recv())

    side = lax.rem(r, 2)
    sibling = r + 1 - 2 * side

    def wanted(s):
        return KS + 1 + s * C + c

    def p_place(kind, row):
        if kind == 0:
            return brow.at[jnp.minimum(row, KS - 1)]
        if kind == 1:
            return brow.at[KS]
        if kind == 2:
            return diag
        return col.at[kind - 3]

    def p_cond(kind, row):
        if kind == 0:
            return True if full else row < KS
        if kind <= 2:
            return row == KS % R
        return row == lax.rem(wanted(kind - 3), R)

    def p_copy(kind, row, place, sem):
        ref = p_place(kind, row)
        return pltpu.make_async_remote_copy(
            src_ref=ref, dst_ref=ref, send_sem=sem, recv_sem=p_recv.at[kind, row],
            device_id={"prow": place}, device_id_type=MESH,
        )

    def t_copy(j, row, place, sem):
        ref = ftri.at[slot(row), j]
        return pltpu.make_async_remote_copy(
            src_ref=ref, dst_ref=ref, send_sem=sem, recv_sem=p_recv.at[3 + CTD + j, row],
            device_id={"prow": place}, device_id_type=MESH,
        )

    def each(kinds, row, act, t_act):
        for kind in kinds:
            if kind == "tiles":
                def one(j, carry):
                    t_act(j)
                    return carry

                lax.fori_loop(0, tiles_of(row), one, 0)
            else:
                when(p_cond(kind, row), lambda kind=kind: act(kind))

    def p_own(kinds, finish):
        def go(copy):
            if finish:
                copy.wait_send()
            else:
                copy.start()

        @pl.loop(0, R // 2)
        def _(d):
            place = jnp.where(d == 0, sibling, lax.rem(r + 2 * d, R))
            each(
                kinds, r,
                lambda kind: go(p_copy(kind, r, place, p_send.at[kind, d])),
                lambda j: go(t_copy(j, r, place, p_send.at[3 + CTD + j, d])),
            )

    def p_pass(kinds):
        @pl.loop(1, R // 2)
        def _(d):
            row = lax.rem(r + R - 2 * d, R)

            def act(kind):
                p_copy(kind, row, sibling, f_send.at[kind, d]).wait_recv()
                p_copy(kind, row, sibling, f_send.at[kind, d]).start()

            def t_act(j):
                t_copy(j, row, sibling, f_send.at[3 + CTD + j, d]).wait_recv()
                t_copy(j, row, sibling, f_send.at[3 + CTD + j, d]).start()

            each(kinds, row, act, t_act)

    def p_pass_done(kinds):
        @pl.loop(1, R // 2)
        def _(d):
            row = lax.rem(r + R - 2 * d, R)
            each(
                kinds, row,
                lambda kind: p_copy(kind, row, sibling, f_send.at[kind, d]).wait_send(),
                lambda j: t_copy(j, row, sibling, f_send.at[3 + CTD + j, d]).wait_send(),
            )

    def p_rest(kinds):
        @pl.loop(0, R // 2)
        def _(d):
            row = 2 * d + 1 - side
            each(
                kinds, row,
                lambda kind: p_copy(kind, row, sibling, f_send.at[kind, 0]).wait_recv(),
                lambda j: t_copy(j, row, sibling, f_send.at[3 + CTD + j, 0]).wait_recv(),
            )

    for kind in range(KF):
        z_start(kind)

    own = pltpu.make_async_copy(factor.at[:, pl.ds(c * A, A)], frow.at[:, c], local_sem)
    own.start()

    def keep_rhs():
        brow[jnp.minimum(r, KS - 1)] = rhs[0]

    when(p_cond(0, r), keep_rhs)

    @pl.when(p_cond(1, r))
    def _():
        brow[KS] = rhs[KS // R]

    for s in range(KF):
        @pl.when(z_cond(s, c))
        def _(s=s):
            ftri[slot(r), s * C + c] = factor[s, first]

    pan_all[pl.ds(c * A, A)] = panel[...]
    for kind in range(KF):
        z_wait_recv(kind)
    z_start(KF)
    p_own(("tiles", 0, 1), False)
    z_wait_recv(KF)
    z_start(KF + 1)

    @pl.when(p_cond(2, r))
    def _():
        diag[...] = pan_all[KS // R]

    for s in range(CTD):
        @pl.when(p_cond(3 + s, r))
        def _(s=s):
            col[s] = pan_all[wanted(s) // R]

    late = tuple(range(2, 3 + CTD))
    p_own(late, False)
    p_pass(("tiles", 0, 1) + late)
    p_rest(late)

    lanes = lax.broadcasted_iota(jnp.int32, (TILE, TILE), 1)
    rows = lax.broadcasted_iota(jnp.int32, (TILE, TILE), 0)
    tri[...] = diag[...]
    inv[...] = jnp.where(lanes == rows, 1.0, 0.0)

    def eliminate(k, carry):
        lane = lanes[0:1]
        row = tri[pl.ds(k, 1), :]
        whole = tri[...]
        pivot = jnp.sum(jnp.where(lane == k, row, 0.0), axis=1, keepdims=True)
        scale = 1.0 / jnp.sqrt(pivot)
        lrow = jnp.where(lane >= k, row * scale, 0.0)
        column = jnp.sum(jnp.where(lanes == k, whole, 0.0), axis=1, keepdims=True)
        lcol = jnp.where(rows[:, 0:1] > k, column * scale, 0.0)
        wrow = inv[pl.ds(k, 1), :] * scale
        tri[...] = whole - lcol * lrow
        inv[...] = inv[...] - lcol * wrow
        tri[pl.ds(k, 1), :] = lrow
        inv[pl.ds(k, 1), :] = wrow
        return carry

    lax.fori_loop(0, TILE, eliminate, 0)
    inv_t[...] = inv[...].T

    p_rest(("tiles", 0, 1))
    p_own((0, 1), True)
    p_pass_done((0, 1))

    def advance(t, carry):
        y[t] = dot(inv_diag[t], brow[t])

        def update(row, carry):
            brow[row] = brow[row] - dot(ftri[row, t], y[t])
            return carry

        return lax.fori_loop(t + 1, KS + 1, update, carry)

    lax.fori_loop(0, KS, advance, 0)
    panel_solution = dot(inv[...], brow[KS])

    scaled = dot(panel[...].reshape(A * TILE, TILE), inv_t[...])
    for a in range(A):
        tile = (c * A + a) * R + r
        panel_out[a] = jnp.where(tile > KS, scaled[a * TILE:(a + 1) * TILE], 0.0)
    brow[KS] = panel_solution

    z_wait_recv(KF + 1)
    own.wait()

    def a_copy(way, source, a):
        place = jnp.clip(c + (1 if way else -1), 0, C - 1)
        ref = forward.at[source * A + a]
        return pltpu.make_async_remote_copy(
            src_ref=ref, dst_ref=ref,
            send_sem=a_send.at[way, source, a], recv_sem=a_recv.at[source, a],
            device_id={"pcol": place}, device_id_type=MESH,
        )

    p_own(late, True)
    p_pass_done(late)
    for s in range(CTD):
        col[s] = dot(col[s], inv_t[...]).T

    def finish(a, carry):
        tile = (c * A + a) * R + r
        total = rhs[c * A + a] - dot(panel_out[a], brow[KS])

        def reach(j, total):
            return total - dot(frow[j // C, lax.rem(j, C), a], y[j])

        total = lax.fori_loop(0, KS, reach, total, unroll=True)
        forward[c * A + a] = total

        @pl.when(tile < KS)
        def _():
            forward[c * A + a] = y[jnp.minimum(tile, KS - 1)]

        @pl.when(tile == KS)
        def _():
            forward[c * A + a] = brow[KS]
            panel_out[a] = tri[...].T

        @pl.when(c < C - 1)
        def _():
            a_copy(1, c, a).start()

        @pl.when(c > 0)
        def _():
            a_copy(0, c, a).start()

        return carry

    lax.fori_loop(0, A, finish, 0)

    def strip_row(i, carry):
        tile = i * R + r
        scaled = jnp.where(tile > KS, dot(pan_all[i], inv_t[...]), 0.0)
        for s in range(CTD):
            strip_out[s, i] = strip[s, i] - dot(scaled, col[s])
        return carry

    steps = (C - 1) * A

    def hop(n, carry):
        lax.fori_loop(n * I // steps, (n + 1) * I // steps, strip_row, 0)
        far = n // A + 1
        a = lax.rem(n, A)

        @pl.when(c - far >= 0)
        def _():
            a_copy(1, c - far, a).wait_recv()

            @pl.when(c < C - 1)
            def _():
                a_copy(1, c - far, a).start()

        @pl.when(c + far < C)
        def _():
            a_copy(0, c + far, a).wait_recv()

            @pl.when(c > 0)
            def _():
                a_copy(0, c + far, a).start()

        return carry

    lax.fori_loop(0, steps, hop, 0)

    for kind in range(KF + 2):
        z_wait_send(kind)
    p_own(("tiles",), True)
    p_pass_done(("tiles",))

    def flush(n, carry):
        source = n // A
        a = lax.rem(n, A)

        @pl.when(jnp.logical_and(source <= c, c < C - 1))
        def _():
            a_copy(1, source, a).wait_send()

        @pl.when(jnp.logical_and(source >= c, c > 0))
        def _():
            a_copy(0, source, a).wait_send()

        return carry

    lax.fori_loop(0, C * A, flush, 0)


def per_device(panel, strip, factor, inv_diag, rhs):
    R = lax.axis_size("prow")
    C = lax.axis_size("pcol")
    A, TILE, _ = panel.shape
    I, _, CTD, _ = strip.shape
    KF = factor.shape[2]
    NR = rhs.shape[2]
    KS = KF * C
    assert KS <= R
    f32 = jnp.float32
    strip = jnp.transpose(strip, (2, 0, 1, 3))
    factor = jnp.transpose(factor, (2, 0, 1, 3))
    kinds = 3 + CTD + KS
    dma = pltpu.SemaphoreType.DMA
    panel_factor, new_strip, forward = pl.pallas_call(
        functools.partial(kernel, R, C),
        out_shape=(
            jax.ShapeDtypeStruct(panel.shape, f32),
            jax.ShapeDtypeStruct(strip.shape, f32),
            jax.ShapeDtypeStruct(rhs.shape, f32),
        ),
        in_specs=[pl.BlockSpec(memory_space=pltpu.VMEM)] * 5,
        out_specs=[pl.BlockSpec(memory_space=pltpu.VMEM)] * 3,
        scratch_shapes=[
            pltpu.VMEM((I, TILE, TILE), f32),
            pltpu.VMEM((TILE, TILE), f32),
            pltpu.VMEM((CTD, TILE, TILE), f32),
            pltpu.VMEM((KS + 1, KS, TILE, TILE), f32),
            pltpu.VMEM((KS + 1, TILE, NR), f32),
            pltpu.VMEM((KS, TILE, NR), f32),
            pltpu.VMEM((KF, C, A, TILE, TILE), f32),
            pltpu.VMEM((TILE, TILE), f32),
            pltpu.VMEM((TILE, TILE), f32),
            pltpu.VMEM((TILE, TILE), f32),
            dma((KF + 2, C - 1)),
            dma((KF + 2, C - 1)),
            dma((kinds, R // 2)),
            dma((kinds, R)),
            dma((kinds, R // 2)),
            dma((2, C, A)),
            dma((C, A)),
            dma,
        ],
        compiler_params=pltpu.CompilerParams(
            collective_id=0, has_side_effects=True, vmem_limit_bytes=56 << 20
        ),
    )(panel, strip, factor, inv_diag, rhs)
    return panel_factor, jnp.transpose(new_strip, (1, 2, 0, 3)), forward


def solution(mesh):
    in_specs = (
        P("pcol", "prow", None),
        P(None, "prow", None, "pcol"),
        P(None, "prow", None, "pcol"),
        P(),
        P(None, "prow", None),
    )
    out_specs = (P("pcol", "prow", None), P(None, "prow", None, "pcol"), P(None, "prow", None))
    return jax.shard_map(
        per_device, mesh=mesh, in_specs=in_specs, out_specs=out_specs, check_vma=False
    )
```

time: 163 us -> 144 us (0.88)
  the two profiles are of different devices: /device:TPU:29 before, /device:TPU:7 now
where the time goes in v2:
time: 144 us
  Pallas kernels  131 us (91%)
  local copies, waits for them, and re-layouts  11.5 us (8%)
    pallas_call x1, Pallas kernels, per_device(): pl.pallas_call(functools.partial(kernel, R, C), out_shape=(jax.ShapeDtype...  131 us
    unnamed x7, local copies, waits for them, and re-layouts  6.72 us
    transpose x1, local copies, waits for them, and re-layouts, per_device(): factor = jnp.transpose(factor, (2, 0, 1, 3))  4.8 us

profile of v2, /device:TPU:7, one launch (start us, length us, event | category | flops | bytes accessed | tf_op | source)
XLA Modules:
  0.0 143.5 jit_solution(12132373387708753116)
XLA Ops:
  0.6 4.8 %copy_bitcast_fusion = (f32[2,16,128,128]{3,2,1,0:T(8,128)}, f32[2,16,128,128]{3,2,1,0:T(8,128)}) fusion(f32[16,128,2,128]{3,2,1,0:T(2,128)} %param.7, f32[16,128,2,128]{3,2,1,0:T(2,128)} %param.6), kind=kLoop, calls=%fused_computation | loop fusion | bytes 8388608 | tf_op jit(solution)/shard_map/transpose | solution.py:397
  5.4 131.3 %shard_map.76 = (f32[4,128,128]{2,1,0:T(8,128)}, f32[2,16,128,128]{3,2,1,0:T(8,128)}, f32[16,128,256]{2,1,0:T(8,128)}) custom-call(f32[4,128,128]{2,1,0:T(8,128)} %panel.1, f32[2,16,128,128]{3,2,1,0:T(8,128)} %get-tuple-element.13.strip, f32[2,16,128,128]{3,2,1,0:T(8,128)} %get-tuple-element.12.factor, f32[8,128,128]{2,1,0:T(8,128)} %inv_diag.1, ...), custom_call_target="tpu_custom_call" | custom-call | tf_op jit(solution)/shard_map/pallas_call | solution.py:400
  136.8 0.0 copy-start.1
  136.8 0.0 copy-start
  136.8 4.7 %copy.10 = f32[16,128,2,128]{3,2,1,0:T(2,128)} copy(f32[16,128,2,128]{3,1,0,2:T(8,128)} %bitcast.5) | data formatting | bytes 4194304
  141.5 0.0 copy-done.1
  141.5 0.7 copy.15
  142.2 0.0 copy-done
  142.2 1.3 copy.16
Async XLA Ops:
  136.8 4.7 %copy-start.1 = (f32[4,128,128]{2,1,0:T(8,128)S(1)}, f32[4,128,128]{2,1,0:T(8,128)}, u32[]{:S(2)}) copy-start(f32[4,128,128]{2,1,0:T(8,128)} %get-tuple-element.17) | copy-start | bytes 786436
  136.8 5.4 %copy-start = (f32[16,128,256]{2,1,0:T(8,128)S(1)}, f32[16,128,256]{2,1,0:T(8,128)}, u32[]{:S(2)}) copy-start(f32[16,128,256]{2,1,0:T(8,128)} %get-tuple-element.19) | copy-start | bytes 6291460

commit v3 on v2

--- a/solution.py
+++ b/solution.py
@@ -67,8 +67,10 @@
             src, dst = factor.at[kind, first], ftri.at[slot(r), kind * C + source]
         elif kind == KF:
             src, dst = panel, pan_all.at[pl.ds(source * A, A)]
+        elif kind == KF + 1:
+            src, dst = factor.at[:, pl.ds(place * A, A)], frow.at[:, source]
         else:
-            src, dst = factor.at[:, pl.ds(place * A, A)], frow.at[:, source]
+            src, dst = panel.at[KS // R % A], diag
         return pltpu.make_async_remote_copy(
             src_ref=src, dst_ref=dst, send_sem=z_send.at[kind, d - 1], recv_sem=z_recv.at[kind, d - 1],
             device_id={"pcol": place}, device_id_type=MESH,
@@ -78,6 +80,8 @@
         return target(row) if full else jnp.where(row <= KS, row, 0)
 
     def z_cond(kind, source):
+        if kind == KF + 2:
+            return jnp.logical_and(r == KS % R, source == KS // R // A)
         return kind * C + source < tiles_of(r) if kind < KF else True
 
     def z_start(kind):
@@ -191,11 +195,12 @@
                 lambda j: t_copy(j, row, sibling, f_send.at[3 + CTD + j, 0]).wait_recv(),
             )
 
+    z_start(KF + 2)
     for kind in range(KF):
         z_start(kind)
 
-    own = pltpu.make_async_copy(factor.at[:, pl.ds(c * A, A)], frow.at[:, c], local_sem)
-    own.start()
+    z_start(KF + 1)
+    z_start(KF)
 
     def keep_rhs():
         brow[jnp.minimum(r, KS - 1)] = rhs[0]
@@ -205,33 +210,29 @@
     @pl.when(p_cond(1, r))
     def _():
         brow[KS] = rhs[KS // R]
+
+    p_own((0, 1), False)
+
+    @pl.when(z_cond(KF + 2, c))
+    def _():
+        diag[...] = panel[KS // R % A]
 
     for s in range(KF):
         @pl.when(z_cond(s, c))
         def _(s=s):
             ftri[slot(r), s * C + c] = factor[s, first]
 
-    pan_all[pl.ds(c * A, A)] = panel[...]
+    z_wait_recv(KF + 2)
+    p_own((2,), False)
     for kind in range(KF):
         z_wait_recv(kind)
-    z_start(KF)
-    p_own(("tiles", 0, 1), False)
-    z_wait_recv(KF)
-    z_start(KF + 1)
-
-    @pl.when(p_cond(2, r))
-    def _():
-        diag[...] = pan_all[KS // R]
-
-    for s in range(CTD):
-        @pl.when(p_cond(3 + s, r))
-        def _(s=s):
-            col[s] = pan_all[wanted(s) // R]
-
-    late = tuple(range(2, 3 + CTD))
-    p_own(late, False)
-    p_pass(("tiles", 0, 1) + late)
-    p_rest(late)
+    p_own(("tiles",), False)
+    own = pltpu.make_async_copy(factor.at[:, pl.ds(c * A, A)], frow.at[:, c], local_sem)
+    own.start()
+    pan_all[pl.ds(c * A, A)] = panel[...]
+    late = tuple(range(3, 3 + CTD))
+    p_pass((2,))
+    p_rest((2,))
 
     lanes = lax.broadcasted_iota(jnp.int32, (TILE, TILE), 1)
     rows = lax.broadcasted_iota(jnp.int32, (TILE, TILE), 0)
@@ -257,7 +258,8 @@
     lax.fori_loop(0, TILE, eliminate, 0)
     inv_t[...] = inv[...].T
 
-    p_rest(("tiles", 0, 1))
+    p_pass((0, 1, "tiles"))
+    p_rest((0, 1, "tiles"))
     p_own((0, 1), True)
     p_pass_done((0, 1))
 
@@ -291,41 +293,50 @@
             device_id={"pcol": place}, device_id_type=MESH,
         )
 
+    def finish(a, carry):
+        tile = (c * A + a) * R + r
+        total = rhs[c * A + a] - dot(panel_out[a], brow[KS])
+
+        def reach(j, total):
+            return total - dot(frow[j // C, lax.rem(j, C), a], y[j])
+
+        total = lax.fori_loop(0, KS, reach, total, unroll=True)
+        forward[c * A + a] = total
+
+        @pl.when(tile < KS)
+        def _():
+            forward[c * A + a] = y[jnp.minimum(tile, KS - 1)]
+
+        @pl.when(tile == KS)
+        def _():
+            forward[c * A + a] = brow[KS]
+            panel_out[a] = tri[...].T
+
+        @pl.when(c < C - 1)
+        def _():
+            a_copy(1, c, a).start()
+
+        @pl.when(c > 0)
+        def _():
+            a_copy(0, c, a).start()
+
+        return carry
+
+    lax.fori_loop(0, A, finish, 0)
+
+    z_wait_recv(KF)
+    for s in range(CTD):
+        @pl.when(p_cond(3 + s, r))
+        def _(s=s):
+            col[s] = pan_all[wanted(s) // R]
+
+    p_own(late, False)
+    p_pass(late)
+    p_rest(late)
     p_own(late, True)
     p_pass_done(late)
     for s in range(CTD):
         col[s] = dot(col[s], inv_t[...]).T
-
-    def finish(a, carry):
-        tile = (c * A + a) * R + r
-        total = rhs[c * A + a] - dot(panel_out[a], brow[KS])
-
-        def reach(j, total):
-            return total - dot(frow[j // C, lax.rem(j, C), a], y[j])
-
-        total = lax.fori_loop(0, KS, reach, total, unroll=True)
-        forward[c * A + a] = total
-
-        @pl.when(tile < KS)
-        def _():
-            forward[c * A + a] = y[jnp.minimum(tile, KS - 1)]
-
-        @pl.when(tile == KS)
-        def _():
-            forward[c * A + a] = brow[KS]
-            panel_out[a] = tri[...].T
-
-        @pl.when(c < C - 1)
-        def _():
-            a_copy(1, c, a).start()
-
-        @pl.when(c > 0)
-        def _():
-            a_copy(0, c, a).start()
-
-        return carry
-
-    lax.fori_loop(0, A, finish, 0)
 
     def strip_row(i, carry):
         tile = i * R + r
@@ -361,10 +372,10 @@
 
     lax.fori_loop(0, steps, hop, 0)
 
-    for kind in range(KF + 2):
+    for kind in range(KF + 3):
         z_wait_send(kind)
-    p_own(("tiles",), True)
-    p_pass_done(("tiles",))
+    p_own((2, "tiles"), True)
+    p_pass_done((2, "tiles"))
 
     def flush(n, carry):
         source = n // A
@@ -417,8 +428,8 @@
             pltpu.VMEM((TILE, TILE), f32),
             pltpu.VMEM((TILE, TILE), f32),
             pltpu.VMEM((TILE, TILE), f32),
-            dma((KF + 2, C - 1)),
-            dma((KF + 2, C - 1)),
+            dma((KF + 3, C - 1)),
+            dma((KF + 3, C - 1)),
             dma((kinds, R // 2)),
             dma((kinds, R)),
             dma((kinds, R // 2)),

time: 144 us -> 131 us (0.910)
  the two profiles are of different devices: /device:TPU:7 before, /device:TPU:0 now
where the time goes in v3:
time: 131 us
  Pallas kernels  119 us (91%)
  local copies, waits for them, and re-layouts  11.5 us (9%)
    pallas_call x1, Pallas kernels, per_device(): pl.pallas_call(functools.partial(kernel, R, C), out_shape=(jax.ShapeDtype...  119 us
    unnamed x7, local copies, waits for them, and re-layouts  6.72 us
    transpose x1, local copies, waits for them, and re-layouts, per_device(): factor = jnp.transpose(factor, (2, 0, 1, 3))  4.8 us

profile of v3, /device:TPU:0, one launch (start us, length us, event | category | flops | bytes accessed | tf_op | source)
XLA Modules:
  0.0 131.2 jit_solution(4765123779965689972)
XLA Ops:
  0.6 4.8 %copy_bitcast_fusion = (f32[2,16,128,128]{3,2,1,0:T(8,128)}, f32[2,16,128,128]{3,2,1,0:T(8,128)}) fusion(f32[16,128,2,128]{3,2,1,0:T(2,128)} %param.7, f32[16,128,2,128]{3,2,1,0:T(2,128)} %param.6), kind=kLoop, calls=%fused_computation | loop fusion | bytes 8388608 | tf_op jit(solution)/shard_map/transpose | solution.py:408
  5.4 119.0 %shard_map.76 = (f32[4,128,128]{2,1,0:T(8,128)}, f32[2,16,128,128]{3,2,1,0:T(8,128)}, f32[16,128,256]{2,1,0:T(8,128)}) custom-call(f32[4,128,128]{2,1,0:T(8,128)} %panel.1, f32[2,16,128,128]{3,2,1,0:T(8,128)} %get-tuple-element.13.strip, f32[2,16,128,128]{3,2,1,0:T(8,128)} %get-tuple-element.12.factor, f32[8,128,128]{2,1,0:T(8,128)} %inv_diag.1, ...), custom_call_target="tpu_custom_call" | custom-call | tf_op jit(solution)/shard_map/pallas_call | solution.py:411
  124.4 0.0 copy-start.1
  124.4 0.0 copy-start
  124.4 4.7 %copy.10 = f32[16,128,2,128]{3,2,1,0:T(2,128)} copy(f32[16,128,2,128]{3,1,0,2:T(8,128)} %bitcast.5) | data formatting | bytes 4194304
  129.1 0.0 copy-done.1
  129.1 0.7 copy.15
  129.8 0.0 copy-done
  129.8 1.3 %copy.16 = f32[16,128,256]{2,1,0:T(8,128)} copy(f32[16,128,256]{2,1,0:T(8,128)S(1)} %copy-done) | data formatting | bytes 4194304
Async XLA Ops:
  124.4 4.7 %copy-start.1 = (f32[4,128,128]{2,1,0:T(8,128)S(1)}, f32[4,128,128]{2,1,0:T(8,128)}, u32[]{:S(2)}) copy-start(f32[4,128,128]{2,1,0:T(8,128)} %get-tuple-element.17) | copy-start | bytes 786436
  124.4 5.4 %copy-start = (f32[16,128,256]{2,1,0:T(8,128)S(1)}, f32[16,128,256]{2,1,0:T(8,128)}, u32[]{:S(2)}) copy-start(f32[16,128,256]{2,1,0:T(8,128)} %get-tuple-element.19) | copy-start | bytes 6291460

commit v4 on v3

--- a/solution.py
+++ b/solution.py
@@ -33,7 +33,7 @@
     c = lax.axis_index("pcol")
     A, TILE, _ = panel.shape
     KF = factor.shape[0]
-    CTD = strip.shape[0]
+    CTD = strip.shape[2]
     I = factor.shape[1]
     KS = KF * C
     NR = rhs.shape[2]
@@ -342,7 +342,7 @@
         tile = i * R + r
         scaled = jnp.where(tile > KS, dot(pan_all[i], inv_t[...]), 0.0)
         for s in range(CTD):
-            strip_out[s, i] = strip[s, i] - dot(scaled, col[s])
+            strip_out[i, :, s, :] = strip[i, :, s, :] - dot(scaled, col[s])
         return carry
 
     steps = (C - 1) * A
@@ -404,7 +404,6 @@
     KS = KF * C
     assert KS <= R
     f32 = jnp.float32
-    strip = jnp.transpose(strip, (2, 0, 1, 3))
     factor = jnp.transpose(factor, (2, 0, 1, 3))
     kinds = 3 + CTD + KS
     dma = pltpu.SemaphoreType.DMA
@@ -441,7 +440,7 @@
             collective_id=0, has_side_effects=True, vmem_limit_bytes=56 << 20
         ),
     )(panel, strip, factor, inv_diag, rhs)
-    return panel_factor, jnp.transpose(new_strip, (1, 2, 0, 3)), forward
+    return panel_factor, new_strip, forward
 
 
 def solution(mesh):

time: 131 us -> 129 us (0.985)
  local copies, waits for them, and re-layouts: 11.5 us -> 9.43 us
    transpose x1 -> x0, local copies, waits for them, and re-layouts: 4.8 us -> none  [per_device(): factor = jnp.transpose(factor, (2, 0, 1, 3))]
    unnamed x7 -> x6, local copies, waits for them, and re-layouts: 6.72 us -> 9.43 us
where the time goes in v4:
time: 129 us
  Pallas kernels  119 us (92%)
  local copies, waits for them, and re-layouts  9.43 us (7%)
    pallas_call x1, Pallas kernels, per_device(): pl.pallas_call(functools.partial(kernel, R, C), out_shape=(jax.ShapeDtype...  119 us
    unnamed x6, local copies, waits for them, and re-layouts  9.43 us

profile of v4, /device:TPU:0, one launch (start us, length us, event | category | flops | bytes accessed | tf_op | source)
XLA Modules:
  0.0 129.1 jit_solution(6573634020777444140)
XLA Ops:
  0.6 3.2 %copy.10 = f32[16,128,2,128]{3,1,0,2:T(8,128)} copy(f32[16,128,2,128]{3,2,1,0:T(2,128)} %param.7) | data formatting | bytes 4194304 | tf_op args[2]
  3.8 119.1 %shard_map.76 = (f32[4,128,128]{2,1,0:T(8,128)}, f32[16,128,2,128]{3,2,1,0:T(2,128)}, f32[16,128,256]{2,1,0:T(8,128)}) custom-call(f32[4,128,128]{2,1,0:T(8,128)} %panel.1, f32[16,128,2,128]{3,2,1,0:T(2,128)} %strip.1, f32[2,16,128,128]{3,2,1,0:T(8,128)} %bitcast.3, f32[8,128,128]{2,1,0:T(8,128)} %inv_diag.1, f32[16,128,256]{2,1,0:T(8,128)} %rhs.1), custom_call_target="tpu_custom_call" | custom-call | tf_op jit(solution)/shard_map/pallas_call | solution.py:410
  122.9 1.7 %copy.14 = f32[4,128,128]{2,1,0:T(8,128)} copy(f32[4,128,128]{2,1,0:T(8,128)} %get-tuple-element.6) | data formatting | bytes 524288
  124.5 0.0 copy-start
  124.5 3.3 %copy.15 = f32[16,128,2,128]{3,2,1,0:T(2,128)} copy(f32[16,128,2,128]{3,2,1,0:T(2,128)} %get-tuple-element.7) | data formatting | bytes 4194304
  127.8 0.0 copy-done
  127.8 1.3 %copy.16 = f32[16,128,256]{2,1,0:T(8,128)} copy(f32[16,128,256]{2,1,0:T(8,128)S(1)} %copy-done) | data formatting | bytes 4194304
Async XLA Ops:
  124.5 3.3 %copy-start = (f32[16,128,256]{2,1,0:T(8,128)S(1)}, f32[16,128,256]{2,1,0:T(8,128)}, u32[]{:S(2)}) copy-start(f32[16,128,256]{2,1,0:T(8,128)} %get-tuple-element.8) | copy-start | bytes 6291460
